TPU v7x, 256 devices: a whole 4x4x8 slice. The times are simulated.
256 devices in a mesh: pair: 16 (over x, y), tensor: 16 (over z, core).
Axes of the slice: x: 4, y: 4, z: 8, core: 2. Of those that a mesh axis runs over, the one named last changes fastest.
Arguments:
- queries: bfloat16 [32, 64, 1024], P('pair', 'tensor'), may hold values from -6 to 6
- documents: bfloat16 [64, 128, 1024], P('pair', 'tensor'), may hold values from -6 to 6
- doc_len: int32 [64], replicated, may hold values from 32 to 128
- route: int32 [16, 16], replicated, may hold values from -1 to 3, as said below
- pair_list: int32 [48, 3], P('pair'), may hold values from 0 to 15, as said below
- attn_gain: float32 [1024], replicated
- w_query: bfloat16 [1024, 8192], P(None, 'tensor')
- w_key: bfloat16 [1024, 8192], P(None, 'tensor')
- w_value: bfloat16 [1024, 8192], P(None, 'tensor'), may hold values from -0.1875 to 0.1875
- w_output: bfloat16 [8192, 1024], P('tensor'), may hold values from -0.5 to 0.5
- ffn_gain: float32 [1024], replicated, may hold values from 0.1 to 1.9
- w_in: bfloat16 [1024, 32768], P(None, 'tensor'), may hold values from -0.1875 to 0.1875
- w_down: bfloat16 [32768, 1024], P('tensor'), may hold values from -0.25 to 0.25
Outputs:
- doc_states: bfloat16 [64, 128, 1024], P('pair', 'tensor')
Inputs may be any that keep to these rules, and one draw needn't show every extreme that they name: route[s, g] is the local index, among the 4 documents of pair index s, of the one document s sends to owner g, or -1 where it sends none; each owner receives exactly min(6, number of pair indices) documents. `pair_list`: rows p * 3 to p * 3 + 2 belong to owner p; column 0 is below 2; columns 1 and 2 differ and name pair indices that send a document to that owner; each document an owner receives fills one or more roles of its pairs.
All inputs are finite; a program needn't handle non-finite values.
Results may differ from a plain program's by a relative error of at most 0.018.
Values may be sent and summed in bfloat16 or wider, within the bound.
A program may use at most 64 MiB of HBM per device.

v0:
```python
import math

import jax
import jax.numpy as jnp
from jax import lax
from jax.sharding import Mesh
from jax.sharding import PartitionSpec as P

HEAD = 128
TENSOR = ("tensor_0", "tensor_1")


def sent_to_all(value, axis):
    copies = jnp.broadcast_to(value, (lax.axis_size(axis), *value.shape))
    return lax.all_to_all(copies, axis, split_axis=0, concat_axis=0, tiled=True)


def in_order(blocks, dim):
    blocks = jnp.moveaxis(blocks, 0, dim)
    dims = blocks.shape
    return blocks.reshape(*dims[:dim], dims[dim] * dims[dim + 1], *dims[dim + 2 :])


def whole_of(value, axes, dim):
    far, near = axes
    first = sent_to_all(value, far)
    blocks = jnp.swapaxes(sent_to_all(first, near), 0, 1)
    return in_order(blocks.reshape(-1, *value.shape), dim)


def in_blocks(value, dim, count):
    dims = value.shape
    blocks = value.reshape(*dims[:dim], count, dims[dim] // count, *dims[dim + 1 :])
    return jnp.moveaxis(blocks, dim, 0)


def sent_and_summed(value, axis, dim):
    count = lax.axis_size(axis)
    blocks = lax.all_to_all(in_blocks(value, dim, count), axis, 0, 0, tiled=True)
    return jnp.sum(blocks.astype(jnp.float32), axis=0)


def sum_by_axis(value, axes, dim):
    far, near = axes
    own = sent_and_summed(in_blocks(value, dim, lax.axis_size(far)), near, dim + 1)
    return jnp.sum(
        lax.all_to_all(own.astype(jnp.bfloat16), far, 0, 0, tiled=True).astype(jnp.float32), axis=0
    )


def rms_norm(values, gain):
    spread = jnp.mean(values * values, -1, keepdims=True)
    return values * lax.rsqrt(spread + 1e-06) * gain


def select_rows(picker, source):
    return jnp.einsum(
        "pn,nld->pld", picker.astype(jnp.bfloat16), source, preferred_element_type=jnp.float32
    ).astype(jnp.bfloat16)


def local(
    queries,
    documents,
    doc_len,
    route,
    pair_list,
    attn_gain,
    w_query,
    w_key,
    w_value,
    w_output,
    ffn_gain,
    w_in,
    w_down,
):
    owners_count = lax.axis_size("pair")
    my_owner = lax.axis_index("pair")
    my_slice = lax.axis_index(TENSOR)
    doc_count, doc_rows, width = documents.shape
    query_rows = queries.shape[1]
    pairs = pair_list.shape[0]
    total_docs = doc_len.shape[0]
    seg_rows = query_rows + 2 * doc_rows
    local_heads = w_query.shape[1] // HEAD
    owner_range = jnp.arange(owners_count, dtype=jnp.int32)
    incoming_route = lax.dynamic_slice_in_dim(route, my_owner, 1, 1)[:, 0]
    outgoing_route = lax.dynamic_slice_in_dim(route, my_owner, 1, 0)[0]
    source_ids = owner_range * doc_count + jnp.maximum(incoming_route, 0)
    first_pick = pair_list[:, 1][:, None] == owner_range[None, :]
    second_pick = pair_list[:, 2][:, None] == owner_range[None, :]
    first_ids = jnp.sum(jnp.where(first_pick, source_ids[None, :], 0), 1)
    second_ids = jnp.sum(jnp.where(second_pick, source_ids[None, :], 0), 1)
    doc_range = jnp.arange(total_docs, dtype=jnp.int32)
    first_global = first_ids[:, None] == doc_range[None, :]
    second_global = second_ids[:, None] == doc_range[None, :]
    first_len = jnp.sum(jnp.where(first_global, doc_len[None, :], 0), 1)
    second_len = jnp.sum(jnp.where(second_global, doc_len[None, :], 0), 1)
    send_pick = outgoing_route[:, None] == jnp.arange(doc_count, dtype=jnp.int32)[None, :]
    outgoing = select_rows(send_pick, documents)
    arrived = lax.all_to_all(outgoing, "pair", split_axis=0, concat_axis=0, tiled=True)
    first_rows = select_rows(first_pick, arrived)
    second_rows = select_rows(second_pick, arrived)
    query_pick = pair_list[:, 0][:, None] == jnp.arange(queries.shape[0], dtype=jnp.int32)[None, :]
    query_rows_sel = select_rows(query_pick, queries)
    own_tokens = jnp.concatenate([query_rows_sel, first_rows, second_rows], 1)
    local_pos = my_slice * doc_rows + jnp.arange(doc_rows, dtype=jnp.int32)
    first_valid = (local_pos[None, :] < first_len[:, None]).astype(jnp.float32)
    second_valid = (local_pos[None, :] < second_len[:, None]).astype(jnp.float32)
    key_index = jnp.arange(lax.axis_size(TENSOR) * seg_rows, dtype=jnp.int32)
    slice_of = key_index // seg_rows
    within = key_index % seg_rows
    first_part = (within >= query_rows) & (within < query_rows + doc_rows)
    second_part = within >= query_rows + doc_rows
    first_doc_pos = slice_of * doc_rows + within - query_rows
    second_doc_pos = slice_of * doc_rows + within - query_rows - doc_rows
    key_ok = (
        (within < query_rows)[None, :]
        | first_part[None, :] & (first_doc_pos[None, :] < first_len[:, None])
        | second_part[None, :] & (second_doc_pos[None, :] < second_len[:, None])
    )
    own_values = own_tokens.astype(jnp.float32)
    normed_own = rms_norm(own_values, attn_gain).astype(jnp.bfloat16)
    normed_all = whole_of(normed_own, ("tensor_0", "tensor_1"), 1)
    rows_all = normed_all.shape[1]
    query_heads = (
        jnp.einsum("prd,de->pre", normed_all, w_query, preferred_element_type=jnp.float32)
        .astype(jnp.bfloat16)
        .reshape(pairs, rows_all, local_heads, HEAD)
    )
    key_heads = (
        jnp.einsum("prd,de->pre", normed_all, w_key, preferred_element_type=jnp.float32)
        .astype(jnp.bfloat16)
        .reshape(pairs, rows_all, local_heads, HEAD)
    )
    value_heads = (
        jnp.einsum("prd,de->pre", normed_all, w_value, preferred_element_type=jnp.float32)
        .astype(jnp.bfloat16)
        .reshape(pairs, rows_all, local_heads, HEAD)
    )
    scores = jnp.einsum(
        "prhd,pshd->phrs", query_heads, key_heads, preferred_element_type=jnp.float32
    ) / math.sqrt(HEAD)
    scores = jnp.where(key_ok[:, None, None, :], scores, jnp.float32(-1e30))
    top = jnp.max(scores, -1, keepdims=True)
    expo = jnp.exp(scores - top)
    probs = (expo / jnp.sum(expo, -1, keepdims=True)).astype(jnp.bfloat16)
    context = jnp.einsum("phrs,pshd->prhd", probs, value_heads, preferred_element_type=jnp.float32)
    context = context.astype(jnp.bfloat16).reshape(pairs, rows_all, local_heads * HEAD)
    hidden_own = own_values + sum_by_axis(
        jnp.einsum("pre,ed->prd", context, w_output, preferred_element_type=jnp.float32).astype(
            jnp.bfloat16
        ),
        ("tensor_0", "tensor_1"),
        1,
    )
    ffn_own = rms_norm(hidden_own, ffn_gain).astype(jnp.bfloat16)
    units = jax.nn.relu(
        jnp.einsum(
            "prd,df->prf",
            whole_of(ffn_own, ("tensor_0", "tensor_1"), 1),
            w_in,
            preferred_element_type=jnp.float32,
        )
    ).astype(jnp.bfloat16)
    ffn_terms = jnp.einsum("prf,fd->prd", units, w_down, preferred_element_type=jnp.float32)
    layer_own = hidden_own + sum_by_axis(
        ffn_terms.astype(jnp.bfloat16), ("tensor_0", "tensor_1"), 1
    )
    first_seg = layer_own[:, query_rows : query_rows + doc_rows] * first_valid[:, :, None]
    second_seg = layer_own[:, query_rows + doc_rows :] * second_valid[:, :, None]
    back = jnp.einsum(
        "pn,pld->nld", first_pick.astype(jnp.float32), first_seg, precision=lax.Precision.HIGHEST
    )
    back = back + jnp.einsum(
        "pn,pld->nld", second_pick.astype(jnp.float32), second_seg, precision=lax.Precision.HIGHEST
    )
    returned = lax.all_to_all(
        back.astype(jnp.bfloat16), "pair", split_axis=0, concat_axis=0, tiled=True
    ).astype(back.dtype)
    home_pick = (outgoing_route[None, :] == jnp.arange(doc_count, dtype=jnp.int32)[:, None]).astype(
        jnp.float32
    )
    totals = jnp.einsum("kn,nld->kld", home_pick, returned, precision=lax.Precision.HIGHEST)
    return totals.astype(jnp.bfloat16)


def solution(mesh):
    torus = Mesh(mesh.devices.reshape(mesh.shape["pair"], 8, 2), ("pair", "tensor_0", "tensor_1"))
    placed = (
        P("pair", TENSOR, None),
        P("pair", TENSOR, None),
        P(),
        P(),
        P("pair", None),
        P(),
        P(None, TENSOR),
        P(None, TENSOR),
        P(None, TENSOR),
        P(TENSOR, None),
        P(),
        P(None, TENSOR),
        P(TENSOR, None),
    )
    return jax.shard_map(
        local, mesh=torus, in_specs=placed, out_specs=P("pair", TENSOR, None), check_vma=False
    )
```

profile of v0, /device:TPU:32, one launch (start us, length us, event | category | flops | bytes accessed | tf_op | source)
XLA Modules:
  0.0 255.9 jit_solution(7772297841919017193)
XLA Ops:
  0.0 0.8 dynamic-slice_bitcast_fusion
  0.8 1.1 convolution_convert_fusion.4
  1.9 0.8 copy.157
  2.8 7.0 %all-to-all-start = ((bf16[16,8,1024]{2,1,0:T(8,128)(2,1)}), bf16[16,8,1024]{2,1,0:T(8,128)(2,1)S(1)}, u32[]{:S(2)}, u32[]{:S(2)}) async-start(bf16[16,8,1024]{2,1,0:T(8,128)(2,1)} %copy.157), calls=%async_computation | async-start | bytes 524288 | tf_op jit(solution)/shard_map/all_to_all | solution.py:101
  9.8 1.0 slice_reduce_fusion.1
  10.8 0.9 fusion.68
  11.8 6.5 %all-to-all-done = bf16[16,8,1024]{2,1,0:T(8,128)(2,1)S(1)} async-done(((bf16[16,8,1024]{2,1,0:T(8,128)(2,1)}), bf16[16,8,1024]{2,1,0:T(8,128)(2,1)S(1)}, u32[]{:S(2)}, u32[]{:S(2)}) %all-to-all-start) | async-done | bytes 262176 | tf_op jit(solution)/shard_map/all_to_all | solution.py:101
  18.3 0.3 fusion.61
  18.6 0.3 fusion.59
  18.9 0.1 fusion.55
  19.1 0.1 fusion.57
  19.2 1.2 broadcast_in_dim.52
  20.4 8.6 %all-to-all-start.1 = ((bf16[8,3,20,1024]{3,2,1,0:T(8,128)(2,1)}), bf16[8,3,20,1024]{3,2,1,0:T(8,128)(2,1)S(1)}, u32[]{:S(2)}, u32[]{:S(2)}) async-start(bf16[8,3,20,1024]{3,2,1,0:T(8,128)(2,1)} %broadcast_in_dim.52), calls=%async_computation.1 | async-start | bytes 2359296 | tf_op jit(solution)/shard_map/all_to_all | solution.py:15
  29.0 0.2 maximum_reduce_fusion
  29.2 0.2 select_reduce_fusion.3
  29.4 0.2 select_reduce_fusion.2
  29.7 28.0 %all-to-all-done.1 = bf16[8,3,20,1024]{3,2,1,0:T(8,128)(2,1)S(1)} async-done(((bf16[8,3,20,1024]{3,2,1,0:T(8,128)(2,1)}), bf16[8,3,20,1024]{3,2,1,0:T(8,128)(2,1)S(1)}, u32[]{:S(2)}, u32[]{:S(2)}) %all-to-all-start.1) | async-done | bytes 983072 | tf_op jit(solution)/shard_map/all_to_all | solution.py:15
  57.7 0.5 copy.162
  58.2 0.3 broadcast_in_dim.53
  58.5 5.3 %all_to_all.50 = bf16[2,8,3,20,1024]{4,1,3,2,0:T(8,128)(2,1)S(1)} all-to-all(bf16[2,8,3,20,1024]{4,1,3,2,0:T(8,128)(2,1)S(1)} %broadcast_in_dim.53), channel_id=1, replica_groups=mesh['pair'=16,'tensor_0'=8,'tensor_1'=2] {'tensor_1'}, dimensions={0} | all-to-all | bytes 3932160 | tf_op jit(solution)/shard_map/all_to_all | solution.py:15
  63.8 2.0 copy.163
  65.9 2.2 reshape.249
  68.1 2.7 %copy.164 = bf16[3,16,20,1024]{3,2,1,0:T(8,128)(2,1)S(1)} copy(bf16[3,16,20,1024]{3,1,2,0:T(8,128)(2,1)} %bitcast.109) | data formatting | bytes 3932160 | tf_op jit(solution)/shard_map/transpose | solution.py:19
  70.7 2.0 reshape.250
  72.7 3.1 %fusion.26 = bf16[3,40,4,8,128]{4,3,2,1,0:T(8,128)(2,1)S(1)} fusion(bf16[3,320,1024]{2,1,0:T(8,128)(2,1)} %reshape.250, bf16[1024,512]{1,0:T(8,128)(2,1)} %param.20), kind=kOutput, calls=%fused_computation.27 | convolution fusion | flops 1007124480 | bytes 3997696 | tf_op jit(solution)/shard_map/prd,de->pre/dot_general | solution.py:132
  75.9 2.1 fusion.25
  78.0 1.2 fusion.24
  79.2 5.7 %fusion.105 = (f32[3,4,320]{2,1,0:T(4,128)S(1)}, f32[3,4,320,320]{2,3,1,0:T(8,128)}) fusion(pred[3,320]{1,0:T(4,128)(4,1)S(1)} %and_or_fusion, bf16[3,40,4,8,128]{4,3,2,1,0:T(8,128)(2,1)S(1)} %fusion.26, bf16[3,40,4,8,128]{4,3,2,1,0:T(8,128)(2,1)} %fusion.25), kind=kOutput, calls=%fused_computation.133 | convolution fusion | flops 319488320 | bytes 6897600 | tf_op jit(solution)/shard_map/sub | solution.py:146
  85.0 3.8 %fusion.23 = bf16[3,4,40,8,128]{4,3,2,1,0:T(8,128)(2,1)S(1)} fusion(f32[3,4,320,320]{2,3,1,0:T(8,128)} %get-tuple-element.17, f32[3,4,320]{2,1,0:T(4,128)S(1)} %get-tuple-element.16, bf16[3,40,4,8,128]{4,3,2,1,0:T(8,128)(2,1)S(1)} %fusion.24), kind=kOutput, calls=%fused_computation.24 | convolution fusion | flops 317521920 | bytes 6896640 | tf_op jit(solution)/shard_map/phrs,pshd->prhd/dot_general | solution.py:148
  88.8 1.2 convolution_convert_fusion
  89.9 1.1 copy.170
  91.0 0.3 copy.171
  91.3 5.3 %all_to_all.51 = bf16[2,8,3,20,1024]{4,1,3,2,0:T(8,128)(2,1)S(1)} all-to-all(bf16[2,8,3,20,1024]{4,1,3,2,0:T(8,128)(2,1)S(1)} %copy.171), channel_id=1, replica_groups=mesh['pair'=16,'tensor_0'=8,'tensor_1'=2] {'tensor_1'}, dimensions={0} | all-to-all | bytes 3932160 | tf_op jit(solution)/shard_map/all_to_all | solution.py:39
  96.6 0.6 reduce_sum.111
  97.2 0.6 copy.173
  97.8 34.6 %all_to_all.52 = bf16[8,3,20,1024]{3,2,1,0:T(8,128)(2,1)S(1)} all-to-all(bf16[8,3,20,1024]{3,2,1,0:T(8,128)(2,1)S(1)} %copy.173), channel_id=1, replica_groups=mesh['pair'=16,'tensor_0'=8,'tensor_1'=2] {'tensor_0'}, dimensions={0} | all-to-all | bytes 1966080 | tf_op jit(solution)/shard_map/all_to_all | solution.py:47
  132.4 1.1 convert_reduce_fusion.1
  133.5 0.1 multiply_reduce_fusion
  133.7 0.1 multiply_convert_fusion
  133.8 0.1 broadcast_in_dim.60
  134.0 34.4 %all_to_all.53 = bf16[8,3,20,1024]{3,2,1,0:T(8,128)(2,1)S(1)} all-to-all(bf16[8,3,20,1024]{3,2,1,0:T(8,128)(2,1)S(1)} %broadcast_in_dim.60), channel_id=1, replica_groups=mesh['pair'=16,'tensor_0'=8,'tensor_1'=2] {'tensor_0'}, dimensions={0} | all-to-all | bytes 1966080 | tf_op jit(solution)/shard_map/all_to_all | solution.py:15
  168.4 0.5 copy.175
  168.9 0.3 broadcast_in_dim.98
  169.2 5.3 %all_to_all.54 = bf16[2,8,3,20,1024]{4,1,3,2,0:T(8,128)(2,1)S(1)} all-to-all(bf16[2,8,3,20,1024]{4,1,3,2,0:T(8,128)(2,1)S(1)} %broadcast_in_dim.98), channel_id=1, replica_groups=mesh['pair'=16,'tensor_0'=8,'tensor_1'=2] {'tensor_1'}, dimensions={0} | all-to-all | bytes 3932160 | tf_op jit(solution)/shard_map/all_to_all | solution.py:15
  174.5 2.0 copy.176
  176.6 2.2 reshape.257
  178.8 2.7 %copy.177 = bf16[3,16,20,1024]{3,2,1,0:T(8,128)(2,1)S(1)} copy(bf16[3,16,20,1024]{3,1,2,0:T(8,128)(2,1)} %bitcast.112) | data formatting | bytes 3932160 | tf_op jit(solution)/shard_map/transpose | solution.py:19
  181.4 2.0 reshape.258
  183.4 12.3 %fusion.15 = bf16[3,320,1024]{2,1,0:T(8,128)(2,1)S(1)} fusion(bf16[2048,1024]{1,0:T(8,128)(2,1)} %param.25, bf16[3,320,1024]{2,1,0:T(8,128)(2,1)} %reshape.258, bf16[1024,2048]{1,0:T(8,128)(2,1)} %param.24), kind=kOutput, calls=%fused_computation.17 | convolution fusion | flops 8057978880 | bytes 12320768 | tf_op jit(solution)/shard_map/prf,fd->prd/dot_general | solution.py:166
  195.7 1.1 copy.178
  196.8 0.3 copy.179
  197.1 5.3 %all_to_all.55 = bf16[2,8,3,20,1024]{4,1,3,2,0:T(8,128)(2,1)S(1)} all-to-all(bf16[2,8,3,20,1024]{4,1,3,2,0:T(8,128)(2,1)S(1)} %copy.179), channel_id=1, replica_groups=mesh['pair'=16,'tensor_0'=8,'tensor_1'=2] {'tensor_1'}, dimensions={0} | all-to-all | bytes 3932160 | tf_op jit(solution)/shard_map/all_to_all | solution.py:39
  202.4 0.6 reduce_sum.114
  203.0 1.6 copy.181
  204.6 5.1 %all-to-all-start.8 = ((bf16[8,3,20,1024]{3,2,1,0:T(8,128)(2,1)}), bf16[8,3,20,1024]{3,2,1,0:T(8,128)(2,1)S(1)}, u32[]{:S(2)}, u32[]{:S(2)}) async-start(bf16[8,3,20,1024]{3,2,1,0:T(8,128)(2,1)} %copy.181), calls=%async_computation.8 | async-start | bytes 2359296 | tf_op jit(solution)/shard_map/all_to_all | solution.py:47
  209.7 30.6 %all-to-all-done.8 = bf16[8,3,20,1024]{3,2,1,0:T(8,128)(2,1)S(1)} async-done(((bf16[8,3,20,1024]{3,2,1,0:T(8,128)(2,1)}), bf16[8,3,20,1024]{3,2,1,0:T(8,128)(2,1)S(1)}, u32[]{:S(2)}, u32[]{:S(2)}) %all-to-all-start.8) | async-done | bytes 983072 | tf_op jit(solution)/shard_map/all_to_all | solution.py:47
  240.3 1.1 convert_reduce_fusion
  241.5 0.1 slice_multiply_fusion
  241.6 0.5 fusion.64
  242.1 0.5 fusion.27
  242.7 0.2 copy.185
  242.8 12.1 %all_to_all.56 = bf16[16,8,1024]{2,1,0:T(8,128)(2,1)S(1)} all-to-all(bf16[16,8,1024]{2,1,0:T(8,128)(2,1)S(1)} %copy.185), channel_id=1, replica_groups=mesh['pair'=16,'tensor_0'=8,'tensor_1'=2] {'pair'}, dimensions={0} | all-to-all | bytes 524288 | tf_op jit(solution)/shard_map/all_to_all | solution.py:178
  255.0 0.3 convolution_convert_fusion.5
  255.2 0.7 copy.187
  (35 shorter events, 0.4 us)
Async XLA Ops:
  0.0 88.7 %copy-start = (bf16[512,1024]{1,0:T(8,128)(2,1)S(1)}, bf16[512,1024]{1,0:T(8,128)(2,1)}, u32[]{:S(2)}) copy-start(bf16[512,1024]{1,0:T(8,128)(2,1)} %param.22) | copy-start | bytes 3145732
  0.0 19.1 %copy-start.6 = (f32[1024]{0:T(1024)S(1)}, f32[1024]{0:T(1024)}, u32[]{:S(2)}) copy-start(f32[1024]{0:T(1024)} %param.18) | copy-start | bytes 12292
  2.8 15.6 %all-to-all-start = ((bf16[16,8,1024]{2,1,0:T(8,128)(2,1)}), bf16[16,8,1024]{2,1,0:T(8,128)(2,1)S(1)}, u32[]{:S(2)}, u32[]{:S(2)}) async-start(bf16[16,8,1024]{2,1,0:T(8,128)(2,1)} %copy.157), calls=%async_computation | async-start | bytes 524288 | tf_op jit(solution)/shard_map/all_to_all | solution.py:101
  19.1 9.9 %copy-start.5 = (s32[16,16]{1,0:T(8,128)S(1)}, s32[16,16]{1,0:T(8,128)}, u32[]{:S(2)}) copy-start(s32[16,16]{1,0:T(8,128)} %param.16) | copy-start | bytes 3076
  19.1 10.3 %copy-start.8 = (s32[64]{0:T(128)S(1)}, s32[64]{0:T(128)}, u32[]{:S(2)}) copy-start(s32[64]{0:T(128)} %param.15) | copy-start | bytes 772
  20.4 37.3 %all-to-all-start.1 = ((bf16[8,3,20,1024]{3,2,1,0:T(8,128)(2,1)}), bf16[8,3,20,1024]{3,2,1,0:T(8,128)(2,1)S(1)}, u32[]{:S(2)}, u32[]{:S(2)}) async-start(bf16[8,3,20,1024]{3,2,1,0:T(8,128)(2,1)} %broadcast_in_dim.52), calls=%async_computation.1 | async-start | bytes 2359296 | tf_op jit(solution)/shard_map/all_to_all | solution.py:15
  72.7 3.2 %copy-start.4 = (bf16[3,320,1024]{2,1,0:T(8,128)(2,1)S(1)}, bf16[3,320,1024]{2,1,0:T(8,128)(2,1)}, u32[]{:S(2)}) copy-start(bf16[3,320,1024]{2,1,0:T(8,128)(2,1)} %reshape.250) | copy-start | bytes 5898244
  72.7 3.2 %copy-start.9 = (bf16[1024,512]{1,0:T(8,128)(2,1)S(1)}, bf16[1024,512]{1,0:T(8,128)(2,1)}, u32[]{:S(2)}) copy-start(bf16[1024,512]{1,0:T(8,128)(2,1)} %param.19) | copy-start | bytes 3145732
  75.9 2.2 copy-start.10
  97.8 35.9 %copy-start.7 = (f32[1024]{0:T(1024)S(1)}, f32[1024]{0:T(1024)}, u32[]{:S(2)}) copy-start(f32[1024]{0:T(1024)} %param.23) | copy-start | bytes 12292
  133.5 34.9 %copy-start.2 = (f32[3,20,1024]{2,1,0:T(8,128)}, f32[3,20,1024]{2,1,0:T(8,128)S(1)}, u32[]{:S(2)}) copy-start(f32[3,20,1024]{2,1,0:T(8,128)S(1)} %convert_reduce_fusion.1) | copy-start | bytes 737284
  204.6 36.9 %copy-start.3 = (f32[3,20,1024]{2,1,0:T(8,128)S(1)}, f32[3,20,1024]{2,1,0:T(8,128)}, u32[]{:S(2)}) copy-start(f32[3,20,1024]{2,1,0:T(8,128)} %copy-done.2) | copy-start | bytes 737284
  204.6 35.7 %all-to-all-start.8 = ((bf16[8,3,20,1024]{3,2,1,0:T(8,128)(2,1)}), bf16[8,3,20,1024]{3,2,1,0:T(8,128)(2,1)S(1)}, u32[]{:S(2)}, u32[]{:S(2)}) async-start(bf16[8,3,20,1024]{3,2,1,0:T(8,128)(2,1)} %copy.181), calls=%async_computation.8 | async-start | bytes 2359296 | tf_op jit(solution)/shard_map/all_to_all | solution.py:47
  241.4 14.5 %copy-start.1 = (bf16[512,1024]{1,0:T(8,128)(2,1)S(1)}, bf16[512,1024]{1,0:T(8,128)(2,1)}, u32[]{:S(2)}) copy-start(bf16[512,1024]{1,0:T(8,128)(2,1)} %param.22) | copy-start | bytes 3145732
where the time goes:
time: 257 us; the launch traced here: 256 us
  blocking collectives  102 us (40%)
  waiting for transfers between devices  65.1 us (25%)
  matrix products  33.4 us (13%)
  local copies, waits for them, and re-layouts  29 us (11%)
  starting transfers between devices  20.7 us (8%)
  other arithmetic  4.83 us (2%)
    all_to_all x3, blocking collectives, sent_to_all(): return lax.all_to_all(copies, axis, split_axis=0, concat_axis=0, tiled=True)  45.1 us
    all_to_all x1, blocking collectives, sum_by_axis(): lax.all_to_all(own.astype(jnp.bfloat16), far, 0, 0, tiled=True)  34.6 us
    all_to_all x1, waiting for transfers between devices, sum_by_axis(): lax.all_to_all(own.astype(jnp.bfloat16), far, 0, 0, tiled=True)  30.6 us
    all_to_all x1, waiting for transfers between devices, sent_to_all(): return lax.all_to_all(copies, axis, split_axis=0, concat_axis=0, tiled=True)  28 us
    dot_general x1, matrix products, local(): jnp.einsum('prf,fd->prd', units, w_down, preferred_element_type=jnp.float32)  12.3 us
    all_to_all x1, blocking collectives, local(): lax.all_to_all(back.astype(jnp.bfloat16), 'pair', split_axis=0, concat_ax...  12.1 us
    all_to_all x2, blocking collectives, sent_and_summed(): lax.all_to_all(in_blocks(value, dim, count), axis, 0, 0, tiled=True)  10.6 us
    all_to_all x1, starting transfers between devices, sent_to_all(): return lax.all_to_all(copies, axis, split_axis=0, concat_axis=0, tiled=True)  8.57 us
  transfers between devices with their start and end apart: 3, of which 3 were waited for; matrix products, arithmetic and copies ran while one was open for 1% of the time, Pallas kernels for 0%

commit v1 on v0

v1 whole, which is shorter than its diff:
```python
import functools
import math

import jax
import jax.numpy as jnp
from jax import lax
from jax.experimental import pallas as pl
from jax.experimental.pallas import tpu as pltpu
from jax.sharding import PartitionSpec as P

HEAD = 128
MESH = pl.DeviceIdType.MESH
BF = jnp.bfloat16
F32 = jnp.float32
ORDER = (0, 1, 2, 0, 1, 2, 0, 0, 1, 0, 1, 2, 0, 1, 2, 0, 1, 2, 0, 1, 2, 0, 1, 2, 0, 1, 2, 0, 0, 1, 2, 1, 0, 1, 2, 0, 2, 1, 2, 0, 1, 2, 1, 2, 2)


def dot(a, b):
    return jnp.dot(a, b, preferred_element_type=F32)


def rms_norm(values, gain):
    spread = jnp.mean(values * values, -1, keepdims=True)
    return values * lax.rsqrt(spread + 1e-06) * gain


def layer_kernel(
    owners,
    ring,
    doc_len,
    route,
    pair_list,
    queries,
    documents,
    attn_gain,
    ffn_gain,
    wq_hbm,
    wk_hbm,
    wv_hbm,
    wo_hbm,
    wi_hbm,
    wd_hbm,
    out,
    wq,
    wk,
    wv,
    wo,
    wi,
    wd,
    sent_docs,
    arrived,
    query_blocks,
    gathered,
    tokens,
    q_buf,
    k_buf,
    v_buf,
    context,
    units,
    mine,
    half_out,
    half_in,
    ring_out,
    ring_in,
    ring_sum,
    results,
    back,
    returned,
    weight_sem,
    pair_send,
    pair_recv,
    gather_send,
    gather_recv,
    core_send,
    core_recv,
    ring_send,
    ring_recv,
):
    me = lax.axis_index("pair")
    place = lax.axis_index("tensor")
    z, core = place // 2, place % 2
    way = 1 - 2 * core
    pairs = pair_list.shape[0]
    docs, rows, width = documents.shape
    query_rows = queries.shape[0]
    block = 2 * rows
    half = ring * block
    q_rows = 2 * ring * query_rows
    heads = q_buf.shape[2] // HEAD
    started = []

    def level(k):
        return (z + way * k + 2 * ring) % ring

    def peer(k):
        return (me, level(k) * 2 + core)

    partner = (me, z * 2 + 1 - core)

    def send(src, dst, send_sem, recv_sem, device):
        copy = pltpu.make_async_remote_copy(
            src_ref=src,
            dst_ref=dst,
            send_sem=send_sem,
            recv_sem=recv_sem,
            device_id=device,
            device_id_type=MESH,
        )
        return copy

    def start(copy):
        copy.start()
        started.append(copy)
        return copy

    weights = []
    for n, (source, target) in enumerate(
        ((wk_hbm, wk), (wv_hbm, wv), (wq_hbm, wq), (wo_hbm, wo), (wi_hbm, wi), (wd_hbm, wd))
    ):
        copy = pltpu.make_async_copy(source, target, weight_sem.at[n])
        copy.start()
        weights.append(copy)

    barrier = pltpu.get_barrier_semaphore()
    for d in range(1, owners):
        pl.semaphore_signal(
            barrier, inc=1, device_id=((me + d) % owners, place), device_id_type=MESH
        )
    for device in (peer(1), peer(-1), peer(2), peer(-2), partner):
        pl.semaphore_signal(barrier, inc=1, device_id=device, device_id_type=MESH)

    for o in range(owners):
        sent_docs[o] = documents[jnp.maximum(route[me, o], 0)]
    arrived[me] = sent_docs[me]
    gain = attn_gain[...]
    query_blocks[z] = rms_norm(queries[...].astype(F32), gain).astype(BF)
    pl.semaphore_wait(barrier, owners + 4)

    def pair_copy(d, src, dst, group):
        there = (me + d) % owners
        return send(
            src.at[there],
            dst.at[me],
            pair_send.at[group, d],
            pair_recv.at[group, d],
            (there, place),
        )

    routed = [start(pair_copy(d, sent_docs, arrived, 0)) for d in range(1, owners)]

    def gather_copies(ref_of, slot):
        def one(n, origin, k):
            part = ref_of(level(origin))
            return send(part, part, gather_send.at[slot, n], gather_recv.at[slot, n], peer(k))

        first = [one(0, 0, 2), one(1, 0, -2), one(2, 0, 1), one(3, 0, -1)]
        second = [one(4, -2, 2), one(5, -2, 1), one(6, 2, -1)]
        return first, second

    def query_part(n):
        return query_blocks.at[n]

    query_first, query_second = gather_copies(query_part, 2 * pairs)
    for copy in query_first:
        start(copy)
    query_first[0].wait_recv()
    query_first[1].wait_recv()
    for copy in query_second:
        start(copy)
    for copy in query_first[2:] + query_second:
        copy.wait_recv()
    query_core = start(
        send(
            query_blocks.at[pl.ds(0, ring)],
            query_blocks.at[pl.ds(ring, ring)],
            core_send.at[4 * pairs],
            core_recv.at[4 * pairs],
            partner,
        )
    )
    weights[0].wait()
    weights[1].wait()
    query_core.wait_recv()
    query_tokens = query_blocks[...].astype(F32).reshape(q_rows, width).astype(BF)
    query_keys = dot(query_tokens, wk[...]).astype(BF)
    query_values = dot(query_tokens, wv[...]).astype(BF)
    for p in range(pairs):
        k_buf[p, pl.ds(2 * half, q_rows)] = query_keys
        v_buf[p, pl.ds(2 * half, q_rows)] = query_values
    for copy in routed:
        copy.wait_recv()

    lane = lax.broadcasted_iota(jnp.int32, (1, 2 * half + q_rows), 1)
    local = lax.broadcasted_iota(jnp.int32, (block, 1), 0)

    def pair_row(p):
        chosen = pair_list[p, 0]
        sources = [pair_list[p, 1], pair_list[p, 2]]
        lengths = [doc_len[s * docs + jnp.maximum(route[s, me], 0)] for s in sources]
        own = jnp.concatenate([arrived[s].astype(F32) for s in sources], 0)
        tokens[p] = own

        def gather(stage, values):
            def part(n):
                return gathered.at[stage, p, pl.ds(pl.multiple_of(n * block, block), block)]

            slot = stage * pairs + p
            gathered[stage, p, pl.ds(pl.multiple_of(z * block, block), block)] = values
            first, second = gather_copies(part, slot)
            for copy in first:
                start(copy)
            yield
            first[0].wait_recv()
            first[1].wait_recv()
            for copy in second:
                start(copy)
            yield
            for copy in first[2:] + second:
                copy.wait_recv()
            other = start(
                send(
                    gathered.at[stage, p, pl.ds(0, half)],
                    gathered.at[stage, p, pl.ds(half, half)],
                    core_send.at[slot],
                    core_recv.at[slot],
                    partner,
                )
            )
            yield
            other.wait_recv()

        def core_copy(stage):
            slot = 2 * pairs + stage * pairs + p
            return send(
                half_out.at[stage, p],
                half_in.at[stage, p],
                core_send.at[slot],
                core_recv.at[slot],
                partner,
            )

        def reduce(stage, other):
            slot = stage * pairs + p
            other.wait_recv()
            total = mine[p] + half_in[stage, p].astype(F32)
            mine[p] = total
            ring_out[stage, p] = total.astype(BF)

            def one(n, origin, k, src=None):
                part = (
                    ring_out.at[
                        stage, p, pl.ds(pl.multiple_of(level(origin) * block, block), block)
                    ]
                    if src is None
                    else src
                )
                return start(
                    send(
                        part,
                        ring_in.at[stage, p, n],
                        ring_send.at[slot, n],
                        ring_recv.at[slot, n],
                        peer(k),
                    )
                )

            first = [one(1, 4, 2), one(0, 3, 1), one(2, -3, -1)]
            near = [one(3, 1, 1), one(4, -1, -1)]

            def summand(origin):
                return mine[p, pl.ds(pl.multiple_of(level(origin) * block, block), block)]

            yield
            for copy in first:
                copy.wait_recv()
            ring_sum[stage, p, 0] = (
                summand(2) + ring_in[stage, p, 0].astype(F32) + ring_in[stage, p, 1].astype(F32)
            ).astype(BF)
            ring_sum[stage, p, 1] = (summand(-2) + ring_in[stage, p, 2].astype(F32)).astype(BF)
            far = [
                one(5, 2, 2, ring_sum.at[stage, p, 0]),
                one(6, -2, -2, ring_sum.at[stage, p, 1]),
            ]
            yield
            for copy in near + far:
                copy.wait_recv()
            total = summand(0)
            for n in range(3, 7):
                total = total + ring_in[stage, p, n].astype(F32)
            return total

        yield from gather(0, rms_norm(own, gain).astype(BF))

        if p == 0:
            weights[2].wait()
        x = gathered[0, p]
        q_buf[p] = dot(x, wq[...]).astype(BF)
        k_buf[p, pl.ds(0, 2 * half)] = dot(x, wk[...]).astype(BF)
        v_buf[p, pl.ds(0, 2 * half)] = dot(x, wv[...]).astype(BF)
        yield
        ring_place = (lane % half) // block
        held_by = jnp.where(lane < half, core, 1 - core)
        position = (ring_place * 2 + held_by) * rows + lane % rows
        limit = jnp.where(lane % block < rows, lengths[0], lengths[1])
        doc_ok = jnp.where(position < limit, 1.0, 0.0)
        query_ok = jnp.where((lane % query_rows) // (query_rows // 2) == chosen, 1.0, 0.0)
        key_ok = jnp.where(lane < 2 * half, doc_ok, query_ok)
        for h in range(heads):
            cols = pl.ds(h * HEAD, HEAD)
            scores = lax.dot_general(
                q_buf[p, :, cols],
                k_buf[p, :, cols],
                (((1,), (1,)), ((), ())),
                preferred_element_type=F32,
            ) * (1.0 / math.sqrt(HEAD))
            scores = jnp.where(key_ok > 0.5, scores, -1e30)
            expo = jnp.exp(scores - jnp.max(scores, -1, keepdims=True))
            probs = (expo * (1.0 / jnp.sum(expo, -1, keepdims=True))).astype(BF)
            context[p, :, cols] = dot(probs, v_buf[p, :, cols]).astype(BF)
        if p == 0:
            weights[3].wait()
        half_out[0, p] = dot(context[p, pl.ds(half, half)], wo[...]).astype(BF)
        other = start(core_copy(0))
        mine[p] = dot(context[p, pl.ds(0, half)], wo[...])
        yield
        hidden = tokens[p] + (yield from reduce(0, other))
        tokens[p] = hidden
        yield from gather(1, rms_norm(hidden, ffn_gain[...]).astype(BF))

        if p == 0:
            weights[4].wait()

        def up(n, _):
            cols = pl.ds(pl.multiple_of(n * 512, 512), 512)
            units[:, cols] = jnp.maximum(dot(gathered[1, p], wi[:, cols]), 0.0).astype(BF)
            return 0

        lax.fori_loop(0, units.shape[1] // 512, up, 0)
        yield
        if p == 0:
            weights[5].wait()

        def down(n, _):
            cols = pl.ds(pl.multiple_of(n * 256, 256), 256)
            term = dot(units[...], wd[:, cols])
            mine[p, :, cols] = term[:half]
            half_out[1, p, :, cols] = term[half:].astype(BF)
            return 0

        lax.fori_loop(0, width // 256, down, 0)
        other = start(core_copy(1))
        yield
        layer_out = tokens[p] + (yield from reduce(1, other))
        position = place * rows + local % rows
        limit = jnp.where(local < rows, lengths[0], lengths[1])
        layer_out = jnp.where(position < limit, layer_out, 0.0)
        results[2 * p] = layer_out[:rows].astype(BF)
        results[2 * p + 1] = layer_out[rows:].astype(BF)

    programs = [pair_row(p) for p in range(pairs)]
    for p in ORDER:
        next(programs[p], None)

    results[2 * pairs] = jnp.zeros((rows, width), BF)
    for o in range(owners):
        role = jnp.int32(2 * pairs)
        for p in range(pairs):
            role = jnp.where(pair_list[p, 1] == o, 2 * p, role)
            role = jnp.where(pair_list[p, 2] == o, 2 * p + 1, role)
        back[o] = results[role]
    returned[me] = back[me]
    home = [start(pair_copy(d, back, returned, 1)) for d in range(1, owners)]
    for copy in home:
        copy.wait_recv()
    for k in range(docs):
        total = jnp.zeros((rows, width), F32)
        for o in range(owners):
            total = total + jnp.where(route[me, o] == k, returned[o].astype(F32), 0.0)
        out[k] = total.astype(BF)
    for copy in started:
        copy.wait_send()


def solution(mesh):
    owners = mesh.shape["pair"]
    ring = mesh.shape["tensor"] // 2
    spread = P("pair", "tensor", None)

    def local(
        queries, documents, doc_len, route, pair_list, attn_gain, wq, wk, wv, wo, ffn_gain, wi, wd
    ):
        pairs = pair_list.shape[0]
        docs, rows, width = documents.shape
        query_rows = queries.shape[0] * queries.shape[1]
        head_width, unit_count = wq.shape[1], wi.shape[1]
        block = 2 * rows
        half = ring * block
        keys = 2 * half + 2 * ring * query_rows
        vmem = pl.BlockSpec(memory_space=pltpu.VMEM)
        smem = pl.BlockSpec(memory_space=pltpu.SMEM)
        hbm = pl.BlockSpec(memory_space=pl.ANY)
        dma = pltpu.SemaphoreType.DMA
        return pl.pallas_call(
            functools.partial(layer_kernel, owners, ring),
            out_shape=jax.ShapeDtypeStruct((docs, rows, width), BF),
            in_specs=[smem] * 3 + [vmem] * 4 + [hbm] * 6,
            out_specs=vmem,
            scratch_shapes=[
                pltpu.VMEM(wq.shape, BF),
                pltpu.VMEM(wk.shape, BF),
                pltpu.VMEM(wv.shape, BF),
                pltpu.VMEM(wo.shape, BF),
                pltpu.VMEM(wi.shape, BF),
                pltpu.VMEM(wd.shape, BF),
                pltpu.VMEM((owners, rows, width), BF),
                pltpu.VMEM((owners, rows, width), BF),
                pltpu.VMEM((2 * ring, query_rows, width), BF),
                pltpu.VMEM((2, pairs, 2 * half, width), BF),
                pltpu.VMEM((pairs, block, width), F32),
                pltpu.VMEM((pairs, 2 * half, head_width), BF),
                pltpu.VMEM((pairs, keys, head_width), BF),
                pltpu.VMEM((pairs, keys, head_width), BF),
                pltpu.VMEM((pairs, 2 * half, head_width), BF),
                pltpu.VMEM((2 * half, unit_count), BF),
                pltpu.VMEM((pairs, half, width), F32),
                pltpu.VMEM((2, pairs, half, width), BF),
                pltpu.VMEM((2, pairs, half, width), BF),
                pltpu.VMEM((2, pairs, half, width), BF),
                pltpu.VMEM((2, pairs, 7, block, width), BF),
                pltpu.VMEM((2, pairs, 2, block, width), BF),
                pltpu.VMEM((2 * pairs + 1, rows, width), BF),
                pltpu.VMEM((owners, rows, width), BF),
                pltpu.VMEM((owners, rows, width), BF),
                dma((6,)),
                dma((2, owners)),
                dma((2, owners)),
                dma((2 * pairs + 1, 7)),
                dma((2 * pairs + 1, 7)),
                dma((4 * pairs + 1,)),
                dma((4 * pairs + 1,)),
                dma((2 * pairs, 7)),
                dma((2 * pairs, 7)),
            ],
            compiler_params=pltpu.CompilerParams(
                collective_id=0, has_side_effects=True, vmem_limit_bytes=60 * 1024 * 1024
            ),
        )(
            doc_len,
            route,
            pair_list,
            queries.reshape(query_rows, width),
            documents,
            attn_gain.reshape(1, width),
            ffn_gain.reshape(1, width),
            wq,
            wk,
            wv,
            wo,
            wi,
            wd,
        )

    placed = (
        spread,
        spread,
        P(),
        P(),
        P("pair", None),
        P(),
        P(None, "tensor"),
        P(None, "tensor"),
        P(None, "tensor"),
        P("tensor", None),
        P(),
        P(None, "tensor"),
        P("tensor", None),
    )
    return jax.shard_map(local, mesh=mesh, in_specs=placed, out_specs=spread, check_vma=False)
```

time: 257 us -> 95.4 us (0.37)
  blocking collectives: 102 us -> 0 us
  Pallas kernels: 0 us -> 91.2 us
  waiting for transfers between devices: 65.1 us -> 0 us
  matrix products: 33.4 us -> 0 us
  local copies, waits for them, and re-layouts: 29 us -> 2.81 us
  starting transfers between devices: 20.7 us -> 0 us
  other arithmetic: 4.83 us -> 0 us
    all_to_all x7 -> x0, blocking collectives: 102 us -> none  [the longest x3 45.1 us: sent_to_all(): return lax.all_to_all(copies, axis, split_axis=0, concat_axis=0, tiled=True)]
    pallas_call x0 -> x1, Pallas kernels: none -> 91.2 us  [local(): pl.pallas_call(functools.partial(layer_kernel, owners, ring), out_shape=j...]
    all_to_all x3 -> x0, waiting for transfers between devices: 65.1 us -> none  [the longest x1 30.6 us: sum_by_axis(): lax.all_to_all(own.astype(jnp.bfloat16), far, 0, 0, tiled=True)]
    dot_general x13 -> x0, matrix products: 27.7 us -> none  [the longest x1 12.3 us: local(): jnp.einsum('prf,fd->prd', units, w_down, preferred_element_type=jnp.float32)]
    all_to_all x3 -> x0, starting transfers between devices: 20.7 us -> none  [the longest x1 8.57 us: sent_to_all(): return lax.all_to_all(copies, axis, split_axis=0, concat_axis=0, tiled=True)]
    transpose x6 -> x0, local copies, waits for them, and re-layouts: 9.92 us -> none  [the longest x2 5.32 us: in_order(): blocks = jnp.moveaxis(blocks, 0, dim)]
    reshape x6 -> x1, local copies, waits for them, and re-layouts: 10.5 us -> 1.33 us  [local(): queries.reshape(query_rows, width)]
    sub x1 -> x0, matrix products: 5.73 us -> none  [local(): expo = jnp.exp(scores - top)]
  transfers between devices with their start and end apart: 3 -> 0, of which waited for: 3 -> 0; matrix products, arithmetic and copies ran while one was open for 1% -> 0% of each run, Pallas kernels for 0% -> 0%
where the time goes in v1:
time: 95.4 us; the launch traced here: 94 us
  Pallas kernels  91.2 us (96%)
  local copies, waits for them, and re-layouts  2.81 us (3%)
    pallas_call x1, Pallas kernels, local(): pl.pallas_call(functools.partial(layer_kernel, owners, ring), out_shape=j...  91.2 us

profile of v1, /device:TPU:32, one launch (start us, length us, event | category | flops | bytes accessed | tf_op | source)
XLA Modules:
  0.0 94.0 jit_solution(12321389955771428380)
XLA Ops:
  0.0 1.3 %reshape.9.queries = bf16[8,1024]{1,0:T(8,128)(2,1)} reshape(bf16[2,4,1024]{2,1,0:T(4,128)(2,1)} %param.13) | data formatting | bytes 32768 | tf_op jit(solution)/shard_map/reshape | solution.py:451
  1.3 91.2 %shard_map.127 = bf16[4,8,1024]{2,1,0:T(8,128)(2,1)} custom-call(s32[64]{0:T(128)} %doc_len.1, s32[16,16]{1,0:T(8,128)} %route.1, s32[3,3]{1,0:T(4,128)} %pair_list.1, bf16[8,1024]{1,0:T(8,128)(2,1)} %reshape.9.queries, bf16[4,8,1024]{2,1,0:T(8,128)(2,1)} %documents.1, f32[1,1024]{1,0:T(1,128)} %bitcast.2, f32[1,1024]{1,0:T(1,128)} %bitcast.3, ...), custom_call_target="tpu_custom_call" | custom-call | tf_op jit(solution)/shard_map/pallas_call | solution.py:403
  92.5 1.5 %copy.15 = bf16[4,8,1024]{2,1,0:T(8,128)(2,1)} copy(bf16[4,8,1024]{2,1,0:T(8,128)(2,1)} %shard_map.127) | data formatting | bytes 131072

commit v2 on v1

--- a/solution.py
+++ b/solution.py
@@ -12,7 +12,7 @@
 MESH = pl.DeviceIdType.MESH
 BF = jnp.bfloat16
 F32 = jnp.float32
-ORDER = (0, 1, 2, 0, 1, 2, 0, 0, 1, 0, 1, 2, 0, 1, 2, 0, 1, 2, 0, 1, 2, 0, 1, 2, 0, 1, 2, 0, 0, 1, 2, 1, 0, 1, 2, 0, 2, 1, 2, 0, 1, 2, 1, 2, 2)
+ORDER = (0, 3, 0, 3, 1, 2, 3, 0, 0, 1, 0, 2, 1, 0, 1, 1, 0, 2, 1, 2, 0, 1, 2, 0, 2, 1, 0, 2, 0, 1, 0, 2, 1, 0, 1, 2, 1, 2, 1, 0, 2, 2, 0, 2, 1, 2, 1, 2)
 
 
 def dot(a, b):
@@ -82,7 +82,8 @@
     way = 1 - 2 * core
     pairs = pair_list.shape[0]
     docs, rows, width = documents.shape
-    query_rows = queries.shape[0]
+    query_count, query_part_rows, _ = queries.shape
+    query_rows = query_count * query_part_rows
     block = 2 * rows
     half = ring * block
     q_rows = 2 * ring * query_rows
@@ -113,6 +114,14 @@
         started.append(copy)
         return copy
 
+    barrier = pltpu.get_barrier_semaphore()
+    for d in range(1, owners):
+        pl.semaphore_signal(
+            barrier, inc=1, device_id=((me + d) % owners, place), device_id_type=MESH
+        )
+    for device in (peer(1), peer(-1), peer(2), peer(-2), partner):
+        pl.semaphore_signal(barrier, inc=1, device_id=device, device_id_type=MESH)
+
     weights = []
     for n, (source, target) in enumerate(
         ((wk_hbm, wk), (wv_hbm, wv), (wq_hbm, wq), (wo_hbm, wo), (wi_hbm, wi), (wd_hbm, wd))
@@ -121,19 +130,12 @@
         copy.start()
         weights.append(copy)
 
-    barrier = pltpu.get_barrier_semaphore()
-    for d in range(1, owners):
-        pl.semaphore_signal(
-            barrier, inc=1, device_id=((me + d) % owners, place), device_id_type=MESH
-        )
-    for device in (peer(1), peer(-1), peer(2), peer(-2), partner):
-        pl.semaphore_signal(barrier, inc=1, device_id=device, device_id_type=MESH)
-
     for o in range(owners):
         sent_docs[o] = documents[jnp.maximum(route[me, o], 0)]
     arrived[me] = sent_docs[me]
     gain = attn_gain[...]
-    query_blocks[z] = rms_norm(queries[...].astype(F32), gain).astype(BF)
+    own_queries = jnp.concatenate([queries[n].astype(F32) for n in range(query_count)], 0)
+    query_blocks[z] = rms_norm(own_queries, gain).astype(BF)
     pl.semaphore_wait(barrier, owners + 4)
 
     def pair_copy(d, src, dst, group):
@@ -163,32 +165,36 @@
     query_first, query_second = gather_copies(query_part, 2 * pairs)
     for copy in query_first:
         start(copy)
-    query_first[0].wait_recv()
-    query_first[1].wait_recv()
-    for copy in query_second:
-        start(copy)
-    for copy in query_first[2:] + query_second:
-        copy.wait_recv()
-    query_core = start(
-        send(
-            query_blocks.at[pl.ds(0, ring)],
-            query_blocks.at[pl.ds(ring, ring)],
-            core_send.at[4 * pairs],
-            core_recv.at[4 * pairs],
-            partner,
-        )
-    )
-    weights[0].wait()
-    weights[1].wait()
-    query_core.wait_recv()
-    query_tokens = query_blocks[...].astype(F32).reshape(q_rows, width).astype(BF)
-    query_keys = dot(query_tokens, wk[...]).astype(BF)
-    query_values = dot(query_tokens, wv[...]).astype(BF)
-    for p in range(pairs):
-        k_buf[p, pl.ds(2 * half, q_rows)] = query_keys
-        v_buf[p, pl.ds(2 * half, q_rows)] = query_values
     for copy in routed:
         copy.wait_recv()
+
+    def query_program():
+        query_first[0].wait_recv()
+        query_first[1].wait_recv()
+        for copy in query_second:
+            start(copy)
+        yield
+        for copy in query_first[2:] + query_second:
+            copy.wait_recv()
+        query_core = start(
+            send(
+                query_blocks.at[pl.ds(0, ring)],
+                query_blocks.at[pl.ds(ring, ring)],
+                core_send.at[4 * pairs],
+                core_recv.at[4 * pairs],
+                partner,
+            )
+        )
+        yield
+        weights[0].wait()
+        weights[1].wait()
+        query_core.wait_recv()
+        query_tokens = query_blocks[...].astype(F32).reshape(q_rows, width).astype(BF)
+        query_keys = dot(query_tokens, wk[...]).astype(BF)
+        query_values = dot(query_tokens, wv[...]).astype(BF)
+        for p in range(pairs):
+            k_buf[p, pl.ds(2 * half, q_rows)] = query_keys
+            v_buf[p, pl.ds(2 * half, q_rows)] = query_values
 
     lane = lax.broadcasted_iota(jnp.int32, (1, 2 * half + q_rows), 1)
     local = lax.broadcasted_iota(jnp.int32, (block, 1), 0)
@@ -303,7 +309,7 @@
         position = (ring_place * 2 + held_by) * rows + lane % rows
         limit = jnp.where(lane % block < rows, lengths[0], lengths[1])
         doc_ok = jnp.where(position < limit, 1.0, 0.0)
-        query_ok = jnp.where((lane % query_rows) // (query_rows // 2) == chosen, 1.0, 0.0)
+        query_ok = jnp.where((lane % query_rows) // query_part_rows == chosen, 1.0, 0.0)
         key_ok = jnp.where(lane < 2 * half, doc_ok, query_ok)
         for h in range(heads):
             cols = pl.ds(h * HEAD, HEAD)
@@ -357,7 +363,7 @@
         results[2 * p] = layer_out[:rows].astype(BF)
         results[2 * p + 1] = layer_out[rows:].astype(BF)
 
-    programs = [pair_row(p) for p in range(pairs)]
+    programs = [pair_row(p) for p in range(pairs)] + [query_program()]
     for p in ORDER:
         next(programs[p], None)
 
@@ -448,7 +454,7 @@
             doc_len,
             route,
             pair_list,
-            queries.reshape(query_rows, width),
+            queries,
             documents,
             attn_gain.reshape(1, width),
             ffn_gain.reshape(1, width),

time: 95.4 us -> 88.7 us (0.930); the launches traced: 94 us -> 88.5 us
  Pallas kernels: 91.2 us -> 87 us
  local copies, waits for them, and re-layouts: 2.81 us -> 1.47 us
    pallas_call x1, Pallas kernels: 91.2 us -> 87 us  [local(): pl.pallas_call(functools.partial(layer_kernel, owners, ring), out_shape=j...]
    reshape x1 -> x0, local copies, waits for them, and re-layouts: 1.33 us -> none  [local(): queries.reshape(query_rows, width)]
where the time goes in v2:
time: 88.7 us; the launch traced here: 88.5 us
  Pallas kernels  87 us (98%)
  local copies, waits for them, and re-layouts  1.47 us (2%)
    pallas_call x1, Pallas kernels, local(): pl.pallas_call(functools.partial(layer_kernel, owners, ring), out_shape=j...  87 us

profile of v2, /device:TPU:32, one launch (start us, length us, event | category | flops | bytes accessed | tf_op | source)
XLA Modules:
  0.0 88.5 jit_solution(8481002132409977386)
XLA Ops:
  0.0 87.0 %shard_map.127 = bf16[4,8,1024]{2,1,0:T(8,128)(2,1)} custom-call(s32[64]{0:T(128)} %doc_len.1, s32[16,16]{1,0:T(8,128)} %route.1, s32[3,3]{1,0:T(4,128)} %pair_list.1, bf16[2,4,1024]{2,1,0:T(4,128)(2,1)} %queries.1, bf16[4,8,1024]{2,1,0:T(8,128)(2,1)} %documents.1, f32[1,1024]{1,0:T(1,128)} %bitcast.2, f32[1,1024]{1,0:T(1,128)} %bitcast.3, ...), custom_call_target="tpu_custom_call" | custom-call | tf_op jit(solution)/shard_map/pallas_call | solution.py:409
  87.0 1.5 %copy.15 = bf16[4,8,1024]{2,1,0:T(8,128)(2,1)} copy(bf16[4,8,1024]{2,1,0:T(8,128)(2,1)} %shard_map.127) | data formatting | bytes 131072

commit v3 on v2

--- a/solution.py
+++ b/solution.py
@@ -98,6 +98,14 @@
 
     partner = (me, z * 2 + 1 - core)
 
+    side = math.isqrt(owners)
+    steps = [(a, b) for a in range(side) for b in range(side)]
+    steps.sort(key=lambda s: -sum(min(n, side - n) for n in s))
+
+    def owner_at(d):
+        a, b = steps[d - 1]
+        return (me // side + a) % side * side + (me % side + b) % side
+
     def send(src, dst, send_sem, recv_sem, device):
         copy = pltpu.make_async_remote_copy(
             src_ref=src,
@@ -116,9 +124,7 @@
 
     barrier = pltpu.get_barrier_semaphore()
     for d in range(1, owners):
-        pl.semaphore_signal(
-            barrier, inc=1, device_id=((me + d) % owners, place), device_id_type=MESH
-        )
+        pl.semaphore_signal(barrier, inc=1, device_id=(owner_at(d), place), device_id_type=MESH)
     for device in (peer(1), peer(-1), peer(2), peer(-2), partner):
         pl.semaphore_signal(barrier, inc=1, device_id=device, device_id_type=MESH)
 
@@ -139,7 +145,7 @@
     pl.semaphore_wait(barrier, owners + 4)
 
     def pair_copy(d, src, dst, group):
-        there = (me + d) % owners
+        there = owner_at(d)
         return send(
             src.at[there],
             dst.at[me],
@@ -165,6 +171,14 @@
     query_first, query_second = gather_copies(query_part, 2 * pairs)
     for copy in query_first:
         start(copy)
+    results[2 * pairs] = jnp.zeros((rows, width), BF)
+    roles = []
+    for o in range(owners):
+        role = jnp.int32(2 * pairs)
+        for p in range(pairs):
+            role = jnp.where(pair_list[p, 1] == o, 2 * p, role)
+            role = jnp.where(pair_list[p, 2] == o, 2 * p + 1, role)
+        roles.append(role)
     for copy in routed:
         copy.wait_recv()
 
@@ -367,15 +381,13 @@
     for p in ORDER:
         next(programs[p], None)
 
-    results[2 * pairs] = jnp.zeros((rows, width), BF)
     for o in range(owners):
-        role = jnp.int32(2 * pairs)
-        for p in range(pairs):
-            role = jnp.where(pair_list[p, 1] == o, 2 * p, role)
-            role = jnp.where(pair_list[p, 2] == o, 2 * p + 1, role)
-        back[o] = results[role]
+        back[o] = results[roles[o]]
     returned[me] = back[me]
+    earlier = len(started)
     home = [start(pair_copy(d, back, returned, 1)) for d in range(1, owners)]
+    for copy in started[:earlier]:
+        copy.wait_send()
     for copy in home:
         copy.wait_recv()
     for k in range(docs):
@@ -383,7 +395,7 @@
         for o in range(owners):
             total = total + jnp.where(route[me, o] == k, returned[o].astype(F32), 0.0)
         out[k] = total.astype(BF)
-    for copy in started:
+    for copy in home:
         copy.wait_send()
 
 

time: 88.7 us -> 87.2 us (0.983)
  Pallas kernels: 87 us -> 85.6 us
    pallas_call x1, Pallas kernels: 87 us -> 85.6 us  [local(): pl.pallas_call(functools.partial(layer_kernel, owners, ring), out_shape=j...]
where the time goes in v3:
time: 87.2 us; the launch traced here: 87.1 us
  Pallas kernels  85.6 us (98%)
  local copies, waits for them, and re-layouts  1.47 us (2%)
    pallas_call x1, Pallas kernels, local(): pl.pallas_call(functools.partial(layer_kernel, owners, ring), out_shape=j...  85.6 us

profile of v3, /device:TPU:32, one launch (start us, length us, event | category | flops | bytes accessed | tf_op | source)
XLA Modules:
  0.0 87.1 jit_solution(10763405051058168902)
XLA Ops:
  0.0 85.6 %shard_map.127 = bf16[4,8,1024]{2,1,0:T(8,128)(2,1)} custom-call(s32[64]{0:T(128)} %doc_len.1, s32[16,16]{1,0:T(8,128)} %route.1, s32[3,3]{1,0:T(4,128)} %pair_list.1, bf16[2,4,1024]{2,1,0:T(4,128)(2,1)} %queries.1, bf16[4,8,1024]{2,1,0:T(8,128)(2,1)} %documents.1, f32[1,1024]{1,0:T(1,128)} %bitcast.2, f32[1,1024]{1,0:T(1,128)} %bitcast.3, ...), custom_call_target="tpu_custom_call" | custom-call | tf_op jit(solution)/shard_map/pallas_call | solution.py:421
  85.6 1.5 %copy.15 = bf16[4,8,1024]{2,1,0:T(8,128)(2,1)} copy(bf16[4,8,1024]{2,1,0:T(8,128)(2,1)} %shard_map.127) | data formatting | bytes 131072

commit v4 on v3

--- a/solution.py
+++ b/solution.py
@@ -27,6 +27,20 @@
 def layer_kernel(
     owners,
     ring,
+    doc_len_hbm,
+    route_hbm,
+    pair_list_hbm,
+    queries_hbm,
+    documents_hbm,
+    attn_gain_hbm,
+    ffn_gain_hbm,
+    wq_hbm,
+    wk_hbm,
+    wv_hbm,
+    wo_hbm,
+    wi_hbm,
+    wd_hbm,
+    out,
     doc_len,
     route,
     pair_list,
@@ -34,13 +48,6 @@
     documents,
     attn_gain,
     ffn_gain,
-    wq_hbm,
-    wk_hbm,
-    wv_hbm,
-    wo_hbm,
-    wi_hbm,
-    wd_hbm,
-    out,
     wq,
     wk,
     wv,
@@ -66,6 +73,7 @@
     results,
     back,
     returned,
+    input_sem,
     weight_sem,
     pair_send,
     pair_recv,
@@ -128,6 +136,21 @@
     for device in (peer(1), peer(-1), peer(2), peer(-2), partner):
         pl.semaphore_signal(barrier, inc=1, device_id=device, device_id_type=MESH)
 
+    inputs = []
+    for n, (source, target) in enumerate(
+        (
+            (route_hbm, route),
+            (documents_hbm, documents),
+            (queries_hbm, queries),
+            (attn_gain_hbm, attn_gain),
+            (pair_list_hbm, pair_list),
+            (doc_len_hbm, doc_len),
+            (ffn_gain_hbm, ffn_gain),
+        )
+    ):
+        copy = pltpu.make_async_copy(source, target, input_sem.at[n])
+        copy.start()
+        inputs.append(copy)
     weights = []
     for n, (source, target) in enumerate(
         ((wk_hbm, wk), (wv_hbm, wv), (wq_hbm, wq), (wo_hbm, wo), (wi_hbm, wi), (wd_hbm, wd))
@@ -136,6 +159,8 @@
         copy.start()
         weights.append(copy)
 
+    for copy in inputs:
+        copy.wait()
     for o in range(owners):
         sent_docs[o] = documents[jnp.maximum(route[me, o], 0)]
     arrived[me] = sent_docs[me]
@@ -415,15 +440,21 @@
         half = ring * block
         keys = 2 * half + 2 * ring * query_rows
         vmem = pl.BlockSpec(memory_space=pltpu.VMEM)
-        smem = pl.BlockSpec(memory_space=pltpu.SMEM)
         hbm = pl.BlockSpec(memory_space=pl.ANY)
         dma = pltpu.SemaphoreType.DMA
         return pl.pallas_call(
             functools.partial(layer_kernel, owners, ring),
-            out_shape=jax.ShapeDtypeStruct((docs, rows, width), BF),
-            in_specs=[smem] * 3 + [vmem] * 4 + [hbm] * 6,
+            out_shape=pltpu.VMEM((docs, rows, width), BF),
+            in_specs=[hbm] * 13,
             out_specs=vmem,
             scratch_shapes=[
+                pltpu.SMEM(doc_len.shape, jnp.int32),
+                pltpu.SMEM(route.shape, jnp.int32),
+                pltpu.SMEM(pair_list.shape, jnp.int32),
+                pltpu.VMEM(queries.shape, BF),
+                pltpu.VMEM(documents.shape, BF),
+                pltpu.VMEM((1, width), F32),
+                pltpu.VMEM((1, width), F32),
                 pltpu.VMEM(wq.shape, BF),
                 pltpu.VMEM(wk.shape, BF),
                 pltpu.VMEM(wv.shape, BF),
@@ -449,6 +480,7 @@
                 pltpu.VMEM((2 * pairs + 1, rows, width), BF),
                 pltpu.VMEM((owners, rows, width), BF),
                 pltpu.VMEM((owners, rows, width), BF),
+                dma((7,)),
                 dma((6,)),
                 dma((2, owners)),
                 dma((2, owners)),

time: 87.2 us -> 85.1 us (0.976)
  Pallas kernels: 85.6 us -> 84.3 us
    pallas_call x1, Pallas kernels: 85.6 us -> 84.3 us  [local(): pl.pallas_call(functools.partial(layer_kernel, owners, ring), out_shape=p...]
where the time goes in v4:
time: 85.1 us; the launch traced here: 84.9 us
  Pallas kernels  84.3 us (99%)
    pallas_call x1, Pallas kernels, local(): pl.pallas_call(functools.partial(layer_kernel, owners, ring), out_shape=p...  84.3 us

profile of v4, /device:TPU:32, one launch (start us, length us, event | category | flops | bytes accessed | tf_op | source)
XLA Modules:
  0.0 84.9 jit_solution(8036367366261171368)
XLA Ops:
  0.0 84.3 %shard_map.127 = bf16[4,8,1024]{2,1,0:T(8,128)(2,1)S(1)} custom-call(s32[64]{0:T(128)} %doc_len_hbm.1, s32[16,16]{1,0:T(8,128)} %route_hbm.1, s32[3,3]{1,0:T(4,128)} %pair_list_hbm.1, bf16[2,4,1024]{2,1,0:T(4,128)(2,1)} %queries_hbm.1, bf16[4,8,1024]{2,1,0:T(8,128)(2,1)} %documents_hbm.1, f32[1,1024]{1,0:T(1,128)} %bitcast.2, f32[1,1024]{1,0:T(1,128)} %bitcast.3, ...), custom_call_target="tpu_custom_call" | custom-call | tf_op jit(solution)/shard_map/pallas_call | solution.py:445
  84.3 0.6 copy.15

commit v5 on v4

--- a/solution.py
+++ b/solution.py
@@ -287,18 +287,16 @@
         def reduce(stage, other):
             slot = stage * pairs + p
             other.wait_recv()
-            total = mine[p] + half_in[stage, p].astype(F32)
-            mine[p] = total
-            ring_out[stage, p] = total.astype(BF)
+
+            def chip_rows(origin):
+                return pl.ds(pl.multiple_of(level(origin) * block, block), block)
+
+            def chip_sum(origin):
+                rows_of = chip_rows(origin)
+                return mine[p, rows_of] + half_in[stage, p, rows_of].astype(F32)
 
             def one(n, origin, k, src=None):
-                part = (
-                    ring_out.at[
-                        stage, p, pl.ds(pl.multiple_of(level(origin) * block, block), block)
-                    ]
-                    if src is None
-                    else src
-                )
+                part = ring_out.at[stage, p, chip_rows(origin)] if src is None else src
                 return start(
                     send(
                         part,
@@ -309,19 +307,23 @@
                     )
                 )
 
+            for origin in (4, 3, -3):
+                ring_out[stage, p, chip_rows(origin)] = chip_sum(origin).astype(BF)
             first = [one(1, 4, 2), one(0, 3, 1), one(2, -3, -1)]
+            for origin in (1, -1):
+                ring_out[stage, p, chip_rows(origin)] = chip_sum(origin).astype(BF)
             near = [one(3, 1, 1), one(4, -1, -1)]
-
-            def summand(origin):
-                return mine[p, pl.ds(pl.multiple_of(level(origin) * block, block), block)]
-
+            for origin in (0, 2, -2):
+                mine[p, chip_rows(origin)] = chip_sum(origin)
             yield
-            for copy in first:
-                copy.wait_recv()
-            ring_sum[stage, p, 0] = (
-                summand(2) + ring_in[stage, p, 0].astype(F32) + ring_in[stage, p, 1].astype(F32)
+            first[2].wait_recv()
+            ring_sum[stage, p, 1] = (
+                mine[p, chip_rows(-2)] + ring_in[stage, p, 2].astype(F32)
             ).astype(BF)
-            ring_sum[stage, p, 1] = (summand(-2) + ring_in[stage, p, 2].astype(F32)).astype(BF)
+            first[1].wait_recv()
+            partial = mine[p, chip_rows(2)] + ring_in[stage, p, 0].astype(F32)
+            first[0].wait_recv()
+            ring_sum[stage, p, 0] = (partial + ring_in[stage, p, 1].astype(F32)).astype(BF)
             far = [
                 one(5, 2, 2, ring_sum.at[stage, p, 0]),
                 one(6, -2, -2, ring_sum.at[stage, p, 1]),
@@ -329,7 +331,7 @@
             yield
             for copy in near + far:
                 copy.wait_recv()
-            total = summand(0)
+            total = mine[p, chip_rows(0)]
             for n in range(3, 7):
                 total = total + ring_in[stage, p, n].astype(F32)
             return total

time: 85.1 us -> 84.9 us (level)
  no operation moved by 1% of the time
where the time goes in v5:
time: 84.9 us; the launch traced here: 84.8 us
  Pallas kernels  84.1 us (99%)
    pallas_call x1, Pallas kernels, local(): pl.pallas_call(functools.partial(layer_kernel, owners, ring), out_shape=p...  84.1 us

profile of v5, /device:TPU:32, one launch (start us, length us, event | category | flops | bytes accessed | tf_op | source)
XLA Modules:
  0.0 84.8 jit_solution(18405687483287823961)
XLA Ops:
  0.0 84.1 %shard_map.127 = bf16[4,8,1024]{2,1,0:T(8,128)(2,1)S(1)} custom-call(s32[64]{0:T(128)} %doc_len_hbm.1, s32[16,16]{1,0:T(8,128)} %route_hbm.1, s32[3,3]{1,0:T(4,128)} %pair_list_hbm.1, bf16[2,4,1024]{2,1,0:T(4,128)(2,1)} %queries_hbm.1, bf16[4,8,1024]{2,1,0:T(8,128)(2,1)} %documents_hbm.1, f32[1,1024]{1,0:T(1,128)} %bitcast.2, f32[1,1024]{1,0:T(1,128)} %bitcast.3, ...), custom_call_target="tpu_custom_call" | custom-call | tf_op jit(solution)/shard_map/pallas_call | solution.py:447
  84.1 0.6 copy.15
